TPU v7x, 32 devices: a whole 2x2x4 slice. The times are simulated.
32 devices in a mesh: ch: 4 (over z), ha: 2 (over x), dp: 4 (over y, core).
Axes of the slice: x: 2, y: 2, z: 4, core: 2. Of those that a mesh axis runs over, the one named last changes fastest.
Arguments:
- features: bfloat16 [384, 4, 4, 4, 128], P('ch', 'dp', None, 'ha'), may hold values from -26 to 26
- frame_count: int32 [4], P('dp'), may hold values from 1 to 4, as said below
- norm1_gain: float32 [384], P('ch'), may hold values from 0.5 to 2
- norm1_shift: float32 [384], P('ch'), may hold values from -3 to 3
- qkv_weight: bfloat16 [384, 1152], replicated, may hold values from -0.51031036 to 0.51031036
- qkv_bias: float32 [1152], replicated, may hold values from -3 to 3
- out_weight: bfloat16 [384, 384], replicated, may hold values from -0.3125 to 0.3125
- out_bias: float32 [384], replicated, may hold values from -3 to 3
- norm2_gain: float32 [384], P('ch'), may hold values from 0.5 to 2
- norm2_shift: float32 [384], P('ch'), may hold values from -3 to 3
- conv_weight: bfloat16 [3, 3, 3, 384, 384], P(None, None, None, 'ch'), may hold values from -0.0625 to 0.0625
- conv_bias: float32 [384], P('ch'), may hold values from -3 to 3
- cotangent: bfloat16 [384, 4, 4, 4, 128], P('ch', 'dp', None, 'ha'), may hold values from -0.0625 to 0.0625
Outputs:
- mixed: bfloat16 [384, 4, 4, 4, 128], P('ch', 'dp', None, 'ha')
- weight_grad: float32 [3, 3, 3, 384, 384], P(None, None, None, 'ch')
Inputs may be any that keep to these rules, and one draw needn't show every extreme that they name: `frame_count`: some clip has all 4 frames valid and some clip only one.
All inputs are finite; a program needn't handle non-finite values.
Results may differ from a plain program's by a relative error of at most 0.015.
Values may be sent and summed in bfloat16 or wider, within the bound.
A program may use at most 64 MiB of HBM per device.

v0:
```python
import jax
import jax.numpy as jnp
from jax import lax
from jax.sharding import PartitionSpec as P

GROUPS = 32
EPS = 1e-06


def padded_2(x, sides, width):
    for axis, dim in sides:
        count, length = (lax.axis_size(axis), x.shape[dim])
        up = [(i, (i + 1) % count) for i in range(count - 1)]
        down = [(j, i) for i, j in up]
        last = lax.slice_in_dim(x, length - width, length, axis=dim)
        leading = lax.slice_in_dim(x, 0, width, axis=dim)
        before = lax.ppermute(last, axis, up)
        after = lax.ppermute(leading, axis, down)
        x = jnp.concatenate([before, x, after], axis=dim)
    return x


def frame_mask(frame_count, frames):
    position = lax.broadcasted_iota(jnp.int32, (frame_count.shape[0], frames), 1)
    return (position < frame_count[:, None]).astype(jnp.float32)


def moments(values, mask, groups):
    chans, clips, frames, rows, cols = values.shape
    data = values.astype(jnp.float32).reshape(groups, chans // groups, clips, frames, rows * cols)
    first = jnp.einsum("gkbfp,bf->gb", data, mask)
    second = jnp.einsum("gkbfp,bf->gb", data * data, mask)
    return (first, second)


def normalize(values, first, second, count, gain, shift, groups):
    chans, clips, frames, rows, cols = values.shape
    mean = first / count[None, :]
    var = second / count[None, :] - mean * mean
    scale = lax.rsqrt(var + EPS)
    data = values.astype(jnp.float32).reshape(groups, chans // groups, clips, frames, rows * cols)
    normed = (data - mean[:, None, :, None, None]) * scale[:, None, :, None, None]
    normed = normed.reshape(values.shape)
    return normed * gain[:, None, None, None, None] + shift[:, None, None, None, None]


def attend(carry, queries, keys, values, scale):
    top, total, acc = carry
    scores = jnp.einsum("itc,isc->its", queries, keys, preferred_element_type=jnp.float32) * scale
    new_top = jnp.max(scores, axis=2)
    factor = jnp.exp(top - new_top)
    weights = jnp.exp(scores - new_top[..., None])
    total = total * factor + jnp.sum(weights, axis=2)
    acc = acc * factor[..., None] + jnp.einsum(
        "its,isc->itc", weights.astype(jnp.bfloat16), values, preferred_element_type=jnp.float32
    )
    return (new_top, total, acc)


def tap_stack(padded, time_tap, frames, rows, cols):
    windows = []
    for row_tap in range(3):
        for col_tap in range(3):
            windows.append(
                padded[
                    :,
                    :,
                    time_tap : time_tap + frames,
                    row_tap : row_tap + rows,
                    col_tap : col_tap + cols,
                ]
            )
    return jnp.concatenate(windows, axis=0)


def butterfly_sum(table, axes):
    steps = []
    for axis in axes:
        size = lax.axis_size(axis)
        for bit in range(size.bit_length() - 1):
            steps.append((axis, bit, size))
    length = table.shape[0]
    unit = (1 << len(steps)) * 8
    padded = -(-length // unit) * unit
    work = jnp.pad(table, ((0, padded - length), (0, 0)))
    for axis, bit, size in steps:
        side = lax.axis_index(axis) >> bit & 1
        halves = work.reshape(2, work.shape[0] // 2, work.shape[1])
        keep = lax.dynamic_index_in_dim(halves, side, keepdims=False)
        send = lax.dynamic_index_in_dim(halves, 1 - side, keepdims=False)
        perm = [(i, i ^ 1 << bit) for i in range(size)]
        got = lax.ppermute(send.astype(jnp.bfloat16), axis, perm)
        work = keep + got.astype(jnp.float32)
    work = work.astype(jnp.bfloat16)
    for axis, bit, size in reversed(steps):
        side = lax.axis_index(axis) >> bit & 1
        perm = [(i, i ^ 1 << bit) for i in range(size)]
        got = lax.ppermute(work, axis, perm)
        pair = jnp.stack([work, got])
        first = lax.dynamic_index_in_dim(pair, side, keepdims=False)
        second = lax.dynamic_index_in_dim(pair, 1 - side, keepdims=False)
        work = jnp.concatenate([first, second], axis=0)
    return work[:length].astype(jnp.float32)


def doubling_sum(values, axis):
    size = lax.axis_size(axis)
    for bit in range(size.bit_length() - 1):
        perm = [(i, i ^ 1 << bit) for i in range(size)]
        got = lax.ppermute(values, axis, perm)
        values = tuple((a + b for a, b in zip(values, got)))
    return values


def body(
    features,
    frame_count,
    norm1_gain,
    norm1_shift,
    qkv_weight,
    qkv_bias,
    out_weight,
    out_bias,
    norm2_gain,
    norm2_shift,
    conv_weight,
    conv_bias,
    cotangent,
):
    chans, clips, frames, rows, cols = features.shape
    groups = GROUPS // lax.axis_size("ch")
    mask = frame_mask(frame_count, frames)
    count = frame_count.astype(jnp.float32) * (chans // groups * rows * lax.axis_size("ha") * cols)
    first, second = moments(features, mask, groups)
    first, second = doubling_sum((first, second), "ha")
    normed = normalize(features, first, second, count, norm1_gain, norm1_shift, groups).astype(
        jnp.bfloat16
    )
    by_frame = lax.all_to_all(normed, "ch", split_axis=2, concat_axis=0, tiled=True)
    width = by_frame.shape[0]
    items = clips * by_frame.shape[2]
    tok_rows = rows * cols
    tokens = by_frame.reshape(width, items, tok_rows)
    queries = lax.dot_general(
        tokens, qkv_weight[:, :width], (((0,), (0,)), ((), ())), preferred_element_type=jnp.float32
    )
    queries = (queries + qkv_bias[:width]).astype(jnp.bfloat16)
    scale = width ** (-0.5)
    start_carry = (
        jnp.full((items, tok_rows), -jnp.inf, jnp.float32),
        jnp.zeros((items, tok_rows), jnp.float32),
        jnp.zeros((items, tok_rows, width), jnp.float32),
    )
    pairs = lax.dot_general(
        tokens, qkv_weight[:, width:], (((0,), (0,)), ((), ())), preferred_element_type=jnp.float32
    )
    pairs = (pairs + qkv_bias[width:]).astype(jnp.bfloat16)
    piece = lax.all_gather(pairs, "ha", axis=1, tiled=True)
    top, total, acc = attend(start_carry, queries, piece[..., :width], piece[..., width:], scale)
    attended = (acc / total[..., None]).astype(jnp.bfloat16)
    projected = lax.dot_general(
        out_weight, attended, (((0,), (2,)), ((), ())), preferred_element_type=jnp.float32
    )
    projected = (projected + out_bias[:, None, None]).astype(jnp.bfloat16).reshape(by_frame.shape)
    update = lax.all_to_all(projected, "ch", split_axis=0, concat_axis=2, tiled=True)
    hidden = (features.astype(jnp.float32) + update.astype(jnp.float32)).astype(jnp.bfloat16)
    first, second = moments(hidden, mask, groups)
    first, second = doubling_sum((first, second), "ha")
    gated = jax.nn.silu(
        normalize(hidden, first, second, count, norm2_gain, norm2_shift, groups)
    ).astype(jnp.bfloat16)
    with_rows = padded_2(gated, (("ha", 3),), 1)
    padded = jnp.pad(with_rows, ((0, 0), (0, 0), (2, 0), (0, 0), (1, 1)))
    stacks = [tap_stack(padded, time_tap, frames, rows, cols) for time_tap in range(3)]
    amount = chans * lax.axis_size("ch")
    summed = jnp.zeros((amount, clips, frames, rows, cols), jnp.float32)
    for time_tap in range(3):
        part = conv_weight[time_tap].reshape(9 * chans, amount)
        summed = summed + lax.dot_general(
            part, stacks[time_tap], (((0,), (0,)), ((), ())), preferred_element_type=jnp.float32
        )
    summed, stacks = lax.optimization_barrier((summed.astype(jnp.bfloat16), stacks))
    shares = lax.axis_size("ch")
    parts = summed.reshape((shares, amount // shares) + summed.shape[1:])
    parts = lax.all_to_all(parts, "ch", split_axis=0, concat_axis=0, tiled=True)
    conv_out = jnp.sum(parts.astype(jnp.float32), axis=0)
    mixed = mask[None, :, :, None, None] * (
        hidden.astype(jnp.float32) + conv_out + conv_bias[:, None, None, None, None]
    )
    mixed = mixed.astype(jnp.bfloat16)
    masked_cot = cotangent * mask.astype(jnp.bfloat16)[None, :, :, None, None]
    full_width = chans * lax.axis_size("ch")
    carry = jnp.zeros((3, 9 * chans, full_width), jnp.float32)
    copies = jnp.broadcast_to(masked_cot[None], (shares,) + masked_cot.shape)
    piece = lax.all_to_all(copies, "ch", split_axis=0, concat_axis=0, tiled=True)
    piece = piece.reshape((shares * chans,) + masked_cot.shape[1:])
    start = jnp.int32(0)
    for time_tap in range(3):
        part = lax.dot_general(
            stacks[time_tap],
            piece,
            (((1, 2, 3, 4), (1, 2, 3, 4)), ((), ())),
            preferred_element_type=jnp.float32,
        )
        carry = lax.dynamic_update_slice(
            carry, part[None], (jnp.int32(time_tap), jnp.int32(0), start)
        )
    weight_grad = butterfly_sum(carry.reshape(27 * chans, full_width), ("dp", "ha"))
    weight_grad = weight_grad.reshape(3, 3, 3, chans, full_width)
    return (mixed, weight_grad)


def solution(mesh):
    placed = (
        P("ch", "dp", None, "ha", None),
        P("dp"),
        P("ch"),
        P("ch"),
        P(),
        P(),
        P(),
        P(),
        P("ch"),
        P("ch"),
        P(None, None, None, "ch", None),
        P("ch"),
        P("ch", "dp", None, "ha", None),
    )
    return jax.shard_map(
        body,
        mesh=mesh,
        in_specs=placed,
        out_specs=(P("ch", "dp", None, "ha", None), P(None, None, None, "ch", None)),
        check_vma=False,
    )
```

profile of v0, /device:TPU:0, one launch (start us, length us, event | category | flops | bytes accessed | tf_op | source)
XLA Modules:
  0.0 152.2 jit_solution(14878665267219705704)
XLA Ops:
  1.3 1.1 fusion.65
  2.8 3.0 %collective-permute-start = (f32[8,1]{0,1:T(1,128)S(1)}, f32[8,1]{0,1:T(1,128)S(1)}, u32[]{:S(2)}, u32[]{:S(2)}) collective-permute-start(f32[8,1]{0,1:T(1,128)S(1)} %convolution_bitcast_fusion.3), channel_id=1, source_target_pairs={{0,4},{4,0},{1,5},{5,1},{2,6},{6,2},{3,7},{7,3},{8,12},{12,8},{9,1... | collective-permute-start | bytes 104 | tf_op jit(solution)/shard_map/ppermute | solution.py:110
  6.1 1.2 collective-permute-done
  7.3 2.3 %collective-permute-done.1 = f32[8,1]{0,1:T(1,128)S(1)} collective-permute-done((f32[8,1]{0,1:T(1,128)S(1)}, f32[8,1]{0,1:T(1,128)S(1)}, u32[]{:S(2)}, u32[]{:S(2)}) %collective-permute-start.1) | collective-permute-done | bytes 64 | tf_op jit(solution)/shard_map/ppermute | solution.py:110
  9.9 1.8 %fusion.91 = bf16[96,1,4,2,128]{4,0,3,1,2:T(8,128)(2,1)} fusion(f32[96]{0:T(128)} %param.16, f32[96]{0:T(128)} %param.15, f32[96]{0:T(128)S(1)} %mul.117, f32[96]{0:T(128)S(1)} %sub.78, bf16[96,1,4,2,128]{4,3,2,1,0:T(2,128)(2,1)} %param.13), kind=kLoop, calls=%fused_computation.119 | loop fusion | flops 589824 | bytes 394752 | tf_op jit(solution)/shard_map/convert_element_type | solution.py:136
  11.8 5.0 %all-to-all-start = ((bf16[96,1,4,2,128]{4,0,3,1,2:T(8,128)(2,1)}), bf16[96,1,4,2,128]{4,0,3,1,2:T(8,128)(2,1)S(1)}, u32[]{:S(2)}, u32[]{:S(2)}) async-start(bf16[96,1,4,2,128]{4,0,3,1,2:T(8,128)(2,1)} %fusion.91), calls=%async_computation | async-start | bytes 393216 | tf_op jit(solution)/shard_map/all_to_all | solution.py:139
  16.8 0.7 slice.123
  17.5 5.5 %all-to-all-done = bf16[96,1,4,2,128]{4,0,3,1,2:T(8,128)(2,1)S(1)} async-done(((bf16[96,1,4,2,128]{4,0,3,1,2:T(8,128)(2,1)}), bf16[96,1,4,2,128]{4,0,3,1,2:T(8,128)(2,1)S(1)}, u32[]{:S(2)}, u32[]{:S(2)}) %all-to-all-start) | async-done | bytes 196640 | tf_op jit(solution)/shard_map/all_to_all | solution.py:139
  23.2 1.5 fusion.37
  24.6 8.7 %all-gather = bf16[512,768]{1,0:T(8,128)(2,1)S(1)} all-gather(bf16[256,768]{1,0:T(8,128)(2,1)S(1)} %fusion.37), channel_id=2, replica_groups=mesh['ch'=4,'ha'=2,'dp'=4] {'ha'}, dimensions={0}, use_global_device_ids=true | all-gather | bytes 1179648 | tf_op jit(solution)/shard_map/all_gather | solution.py:158
  33.3 1.6 %fusion.119 = (f32[256]{0:T(256)S(1)}, f32[256,512]{1,0:T(8,128)S(1)}) fusion(bf16[1,512,768]{2,1,0:T(8,128)(2,1)S(1)} %bitcast.223, bf16[384,1152]{1,0:T(8,128)(2,1)} %param.17, f32[384]{0:T(512)S(1)} %slice-done, bf16[48,8,2,128]{3,2,1,0:T(2,128)(2,1)S(1)} %bitcast.232), kind=kOutput, calls=%fused_computation.180 | convolution fusion | flops 176619264 | bytes 1412096 | tf_op jit(solution)/shard_map/itc,isc->its/dot_general | solution.py:49
  35.2 0.6 fusion.46
  35.7 0.9 copy.28
  36.6 3.4 %all-to-all-start.1 = ((bf16[384,1,1,2,128]{4,3,2,1,0:T(2,128)(2,1)}), bf16[384,1,1,2,128]{4,3,2,1,0:T(2,128)(2,1)S(1)}, u32[]{:S(2)}, u32[]{:S(2)}) async-start(bf16[384,1,1,2,128]{4,3,2,1,0:T(2,128)(2,1)} %copy.28), calls=%async_computation.1 | async-start | bytes 393216 | tf_op jit(solution)/shard_map/all_to_all | solution.py:165
  40.3 5.9 %all-to-all-done.1 = bf16[384,1,1,2,128]{4,3,2,1,0:T(2,128)(2,1)S(1)} async-done(((bf16[384,1,1,2,128]{4,3,2,1,0:T(2,128)(2,1)}), bf16[384,1,1,2,128]{4,3,2,1,0:T(2,128)(2,1)S(1)}, u32[]{:S(2)}, u32[]{:S(2)}) %all-to-all-start.1) | async-done | bytes 196640 | tf_op jit(solution)/shard_map/all_to_all | solution.py:165
  46.2 1.0 broadcast_in_dim.17
  47.2 3.5 %all-to-all-start.3 = ((bf16[4,96,1,4,2,128]{5,1,4,3,2,0:T(8,128)(2,1)}), bf16[4,96,1,4,2,128]{5,1,4,3,2,0:T(8,128)(2,1)S(1)}, u32[]{:S(2)}, u32[]{:S(2)}) async-start(bf16[4,96,1,4,2,128]{5,1,4,3,2,0:T(8,128)(2,1)} %broadcast_in_dim.17), calls=%async_computation.3 | async-start | bytes 1572864 | tf_op jit(solution)/shard_map/all_to_all | solution.py:195
  51.3 0.6 collective-permute-start.2
  52.1 1.5 collective-permute-start.3
  53.6 1.2 collective-permute-done.2
  54.9 0.8 collective-permute-done.3
  56.0 0.3 fusion.75
  56.4 3.4 %collective-permute-start.4 = (bf16[96,1,4,1,128]{4,0,3,2,1:T(8,128)(2,1)S(1)}, bf16[96,1,4,1,128]{4,0,3,2,1:T(8,128)(2,1)S(1)}, u32[]{:S(2)}, u32[]{:S(2)}) collective-permute-start(bf16[96,1,4,1,128]{4,0,3,2,1:T(8,128)(2,1)S(1)} %get-tuple-element.61), channel_id=1, source_target_pairs={{0,4},{1,5},{2,6},{3,7},{8,12},{9,13},{10,14},{11,15},{16,20},{17,... | collective-permute-start | bytes 294920 | tf_op jit(solution)/shard_map/ppermute | solution.py:17
  59.8 1.5 collective-permute-start.5
  61.3 2.6 %fusion.117 = (bf16[1,3,3,96,384]{4,3,2,1,0:T(8,128)(2,1)}, bf16[1,3,3,96,384]{4,3,2,1,0:T(8,128)(2,1)S(1)}, bf16[1,3,3,96,384]{4,3,2,1,0:T(8,128)(2,1)S(1)}) fusion(bf16[3,3,3,96,384]{4,3,2,1,0:T(8,128)(2,1)} %param.23), kind=kLoop, calls=%fused_computation.178 | loop fusion | bytes 3981312 | tf_op jit(solution)/shard_map/slice | solution.py:178
  63.9 2.5 %collective-permute-done.5 = bf16[96,1,4,1,128]{4,0,3,2,1:T(8,128)(2,1)S(1)} collective-permute-done((bf16[96,1,4,1,128]{4,0,3,2,1:T(8,128)(2,1)S(1)}, bf16[96,1,4,1,128]{4,0,3,2,1:T(8,128)(2,1)S(1)}, u32[]{:S(2)}, u32[]{:S(2)}) %collective-permute-start.5) | collective-permute-done | bytes 98336 | tf_op jit(solution)/shard_map/ppermute | solution.py:18
  66.3 0.4 fusion.41
  67.6 0.3 slice_dynamic-update-slice_fusion.9
  68.1 0.4 constant_dynamic-update-slice_fusion
  68.5 0.3 slice_dynamic-update-slice_fusion.7
  69.3 1.2 fusion.13
  70.5 1.2 fusion.15
  71.8 1.3 fusion.34
  73.1 2.6 %fusion.19 = f32[1,864,384]{2,1,0:T(8,128)S(1)} fusion(bf16[384,4,2,128]{3,0,2,1:T(8,128)(2,1)S(1)} %bitcast.225, bf16[864,1,4,2,128]{4,0,3,2,1:T(8,128)(2,1)} %copy-done.7), kind=kOutput, calls=%fused_computation.29 | convolution fusion | flops 679477248 | bytes 3883008 | tf_op jit(solution)/shard_map/dot_general | solution.py:199
  75.7 0.3 dynamic_update_slice.9
  76.0 1.2 copy-done.6
  77.2 1.1 fusion.25
  78.3 0.4 copy-done.4
  78.7 1.1 fusion.31
  79.8 0.3 pad.10
  80.1 1.9 %copy-done.1 = f32[2624,384]{1,0:T(8,128)} copy-done((f32[2624,384]{1,0:T(8,128)}, f32[2624,384]{1,0:T(8,128)S(1)}, u32[]{:S(2)}) %copy-start.1) | copy-done | bytes 4030488
  82.2 2.7 %collective-permute-done.6 = bf16[1312,384]{1,0:T(8,128)(2,1)} collective-permute-done((bf16[1312,384]{1,0:T(8,128)(2,1)S(1)}, bf16[1312,384]{1,0:T(8,128)(2,1)}, u32[]{:S(2)}, u32[]{:S(2)}) %collective-permute-start.6) | collective-permute-done | bytes 1007648 | tf_op jit(solution)/shard_map/ppermute | solution.py:92
  84.9 2.0 %bitcast_add_fusion = f32[1312,384]{1,0:T(8,128)S(1)} fusion(bf16[1312,384]{1,0:T(8,128)(2,1)} %collective-permute-done.6, f32[2,1312,384]{2,1,0:T(8,128)} %bitcast.214, s32[]{:T(128)S(6)} %select_n.30), kind=kLoop, calls=%fused_computation.12 | loop fusion | flops 1007616 | bytes 5038084 | tf_op jit(solution)/shard_map/add | solution.py:93
  86.9 0.8 fusion.53
  87.8 1.5 %collective-permute-start.7 = (bf16[656,384]{1,0:T(8,128)(2,1)}, bf16[656,384]{1,0:T(8,128)(2,1)}, u32[]{:S(2)}, u32[]{:S(2)}) collective-permute-start(bf16[656,384]{1,0:T(8,128)(2,1)} %fusion.53), channel_id=1, source_target_pairs={{0,2},{1,3},{2,0},{3,1},{4,6},{5,7},{6,4},{7,5},{8,10},{9,11},{10,... | collective-permute-start | bytes 1511432 | tf_op jit(solution)/shard_map/ppermute | solution.py:92
  89.3 12.3 %collective-permute-done.7 = bf16[656,384]{1,0:T(8,128)(2,1)} collective-permute-done((bf16[656,384]{1,0:T(8,128)(2,1)}, bf16[656,384]{1,0:T(8,128)(2,1)}, u32[]{:S(2)}, u32[]{:S(2)}) %collective-permute-start.7) | collective-permute-done | bytes 503840 | tf_op jit(solution)/shard_map/ppermute | solution.py:92
  101.6 2.1 %bitcast_add_fusion.1 = f32[656,384]{1,0:T(8,128)} fusion(bf16[656,384]{1,0:T(8,128)(2,1)} %collective-permute-done.7, f32[2,656,384]{2,1,0:T(8,128)S(1)} %bitcast.217, s32[]{:T(128)S(6)} %select_n.32), kind=kLoop, calls=%fused_computation.64 | loop fusion | flops 503808 | bytes 2519044 | tf_op jit(solution)/shard_map/add | solution.py:93
  103.7 1.1 fusion.86
  105.0 7.1 %collective-permute-done.8 = bf16[328,384]{1,0:T(8,128)(2,1)S(1)} collective-permute-done((bf16[328,384]{1,0:T(8,128)(2,1)S(1)}, bf16[328,384]{1,0:T(8,128)(2,1)S(1)}, u32[]{:S(2)}, u32[]{:S(2)}) %collective-permute-start.8) | collective-permute-done | bytes 251936 | tf_op jit(solution)/shard_map/ppermute | solution.py:92
  112.1 1.1 fusion.58
  113.2 0.4 collective-permute-start.9
  113.5 6.1 %collective-permute-done.9 = bf16[328,384]{1,0:T(8,128)(2,1)S(1)} collective-permute-done((bf16[328,384]{1,0:T(8,128)(2,1)S(1)}, bf16[328,384]{1,0:T(8,128)(2,1)S(1)}, u32[]{:S(2)}, u32[]{:S(2)}) %collective-permute-start.9) | collective-permute-done | bytes 251936 | tf_op jit(solution)/shard_map/ppermute | solution.py:98
  119.9 1.1 pad_maximum_fusion.2
  120.9 1.5 %collective-permute-start.10 = (bf16[656,384]{1,0:T(8,128)(2,1)}, bf16[656,384]{1,0:T(8,128)(2,1)}, u32[]{:S(2)}, u32[]{:S(2)}) collective-permute-start(bf16[656,384]{1,0:T(8,128)(2,1)} %get-tuple-element.57), channel_id=1, source_target_pairs={{0,2},{1,3},{2,0},{3,1},{4,6},{5,7},{6,4},{7,5},{8,10},{9,11},{10,... | collective-permute-start | bytes 1511432 | tf_op jit(solution)/shard_map/ppermute | solution.py:98
  122.5 0.4 copy.31
  122.9 1.0 copy.32
  123.9 5.1 %all-to-all-start.2 = ((bf16[4,96,1,4,2,128]{5,1,4,3,2,0:T(8,128)(2,1)}), bf16[4,96,1,4,2,128]{5,1,4,3,2,0:T(8,128)(2,1)S(1)}, u32[]{:S(2)}, u32[]{:S(2)}) async-start(bf16[4,96,1,4,2,128]{5,1,4,3,2,0:T(8,128)(2,1)} %copy.32), calls=%async_computation.2 | async-start | bytes 1572864 | tf_op jit(solution)/shard_map/all_to_all | solution.py:185
  128.9 3.3 %collective-permute-done.10 = bf16[656,384]{1,0:T(8,128)(2,1)} collective-permute-done((bf16[656,384]{1,0:T(8,128)(2,1)}, bf16[656,384]{1,0:T(8,128)(2,1)}, u32[]{:S(2)}, u32[]{:S(2)}) %collective-permute-start.10) | collective-permute-done | bytes 503840 | tf_op jit(solution)/shard_map/ppermute | solution.py:98
  132.2 1.5 fusion.57
  133.7 1.1 pad_maximum_fusion.1
  134.8 11.7 %all-to-all-done.2 = bf16[4,96,1,4,2,128]{5,1,4,3,2,0:T(8,128)(2,1)S(1)} async-done(((bf16[4,96,1,4,2,128]{5,1,4,3,2,0:T(8,128)(2,1)}), bf16[4,96,1,4,2,128]{5,1,4,3,2,0:T(8,128)(2,1)S(1)}, u32[]{:S(2)}, u32[]{:S(2)}) %all-to-all-start.2) | async-done | bytes 786464 | tf_op jit(solution)/shard_map/all_to_all | solution.py:185
  146.7 0.8 copy.35
  147.6 2.0 %fusion.51 = (bf16[1312,384]{1,0:T(8,128)(2,1)S(1)}, bf16[1312,384]{1,0:T(8,128)(2,1)S(1)}) fusion(s32[]{:T(128)S(6)} %select_n.30, bf16[1,1312,384]{2,1,0:T(8,128)(2,1)S(1)} %get-tuple-element.54, bf16[1,1312,384]{2,1,0:T(8,128)(2,1)} %bitcast.78, s32[]{:T(128)S(6)} %select_n.31), kind=kLoop, calls=%fused_computation.62 | loop fusion | flops 1007616 | bytes 4030472 | tf_op jit(solution)/shard_map/jit(dynamic_index_in_dim)/squeeze | solution.py:100
  149.8 2.4 %convert.5 = f32[3,3,3,96,384]{4,3,2,1,0:T(8,128)} convert(bf16[3,3,3,96,384]{4,3,2,1,0:T(8,128)(2,1)S(1)} %bitcast.215) | non-fusion elementwise | flops 995328 | bytes 5971968 | tf_op jit(solution)/shard_map/reshape | solution.py:209
  (84 shorter events, 5.4 us)
Async XLA Ops:
  0.6 34.5 %copy-start = (bf16[384,384]{1,0:T(8,128)(2,1)S(1)}, bf16[384,384]{1,0:T(8,128)(2,1)}, u32[]{:S(2)}) copy-start(bf16[384,384]{1,0:T(8,128)(2,1)} %param.19) | copy-start | bytes 884740
  2.8 4.5 %collective-permute-start = (f32[8,1]{0,1:T(1,128)S(1)}, f32[8,1]{0,1:T(1,128)S(1)}, u32[]{:S(2)}, u32[]{:S(2)}) collective-permute-start(f32[8,1]{0,1:T(1,128)S(1)} %convolution_bitcast_fusion.3), channel_id=1, source_target_pairs={{0,4},{4,0},{1,5},{5,1},{2,6},{6,2},{3,7},{7,3},{8,12},{12,8},{9,1... | collective-permute-start | bytes 104 | tf_op jit(solution)/shard_map/ppermute | solution.py:110
  6.0 3.6 %collective-permute-start.1 = (f32[8,1]{0,1:T(1,128)S(1)}, f32[8,1]{0,1:T(1,128)S(1)}, u32[]{:S(2)}, u32[]{:S(2)}) collective-permute-start(f32[8,1]{0,1:T(1,128)S(1)} %convolution_bitcast_fusion.2), channel_id=1, source_target_pairs={{0,4},{4,0},{1,5},{5,1},{2,6},{6,2},{3,7},{7,3},{8,12},{12,8},{9,1... | collective-permute-start | bytes 104 | tf_op jit(solution)/shard_map/ppermute | solution.py:110
  11.8 21.5 %slice-start = ((f32[1152]{0:T(1024)}), f32[384]{0:T(512)S(1)}, s32[]{:S(2)}) async-start(f32[1152]{0:T(1024)} %param.18), calls=%async_computation.4 | async-start | bytes 4096 | tf_op jit(solution)/shard_map/slice | solution.py:147
  11.8 11.3 %all-to-all-start = ((bf16[96,1,4,2,128]{4,0,3,1,2:T(8,128)(2,1)}), bf16[96,1,4,2,128]{4,0,3,1,2:T(8,128)(2,1)S(1)}, u32[]{:S(2)}, u32[]{:S(2)}) async-start(bf16[96,1,4,2,128]{4,0,3,1,2:T(8,128)(2,1)} %fusion.91), calls=%async_computation | async-start | bytes 393216 | tf_op jit(solution)/shard_map/all_to_all | solution.py:139
  24.6 10.5 %copy-start.14 = (f32[384]{0:T(512)S(1)}, f32[384]{0:T(512)}, u32[]{:S(2)}) copy-start(f32[384]{0:T(512)} %param.20) | copy-start | bytes 4612
  35.2 4.8 %copy-start.10 = (bf16[96,1,4,2,128]{4,3,2,1,0:T(2,128)(2,1)S(1)}, bf16[96,1,4,2,128]{4,3,2,1,0:T(2,128)(2,1)}, u32[]{:S(2)}) copy-start(bf16[96,1,4,2,128]{4,3,2,1,0:T(2,128)(2,1)} %param.25) | copy-start | bytes 589828
  36.6 9.6 %all-to-all-start.1 = ((bf16[384,1,1,2,128]{4,3,2,1,0:T(2,128)(2,1)}), bf16[384,1,1,2,128]{4,3,2,1,0:T(2,128)(2,1)S(1)}, u32[]{:S(2)}, u32[]{:S(2)}) async-start(bf16[384,1,1,2,128]{4,3,2,1,0:T(2,128)(2,1)} %copy.28), calls=%async_computation.1 | async-start | bytes 393216 | tf_op jit(solution)/shard_map/all_to_all | solution.py:165
  40.2 10.5 %copy-start.9 = (bf16[96,1,4,2,128]{4,3,2,1,0:T(2,128)(2,1)S(1)}, bf16[96,1,4,2,128]{4,3,2,1,0:T(2,128)(2,1)}, u32[]{:S(2)}) copy-start(bf16[96,1,4,2,128]{4,3,2,1,0:T(2,128)(2,1)} %param.13) | copy-start | bytes 589828
  40.3 15.8 %copy-start.11 = (f32[96]{0:T(128)S(1)}, f32[96]{0:T(128)}, u32[]{:S(2)}) copy-start(f32[96]{0:T(128)} %param.22) | copy-start | bytes 1156
  40.3 15.7 %copy-start.12 = (f32[96]{0:T(128)S(1)}, f32[96]{0:T(128)}, u32[]{:S(2)}) copy-start(f32[96]{0:T(128)} %param.21) | copy-start | bytes 1156
  47.2 25.8 %all-to-all-start.3 = ((bf16[4,96,1,4,2,128]{5,1,4,3,2,0:T(8,128)(2,1)}), bf16[4,96,1,4,2,128]{5,1,4,3,2,0:T(8,128)(2,1)S(1)}, u32[]{:S(2)}, u32[]{:S(2)}) async-start(bf16[4,96,1,4,2,128]{5,1,4,3,2,0:T(8,128)(2,1)} %broadcast_in_dim.17), calls=%async_computation.3 | async-start | bytes 1572864 | tf_op jit(solution)/shard_map/all_to_all | solution.py:195
  51.3 3.6 %collective-permute-start.2 = (f32[8,1]{0,1:T(1,128)S(1)}, f32[8,1]{0,1:T(1,128)S(1)}, u32[]{:S(2)}, u32[]{:S(2)}) collective-permute-start(f32[8,1]{0,1:T(1,128)S(1)} %convolution_bitcast_fusion.1), channel_id=1, source_target_pairs={{0,4},{4,0},{1,5},{5,1},{2,6},{6,2},{3,7},{7,3},{8,12},{12,8},{9,1... | collective-permute-start | bytes 104 | tf_op jit(solution)/shard_map/ppermute | solution.py:110
  52.1 3.6 %collective-permute-start.3 = (f32[8,1]{0,1:T(1,128)S(1)}, f32[8,1]{0,1:T(1,128)S(1)}, u32[]{:S(2)}, u32[]{:S(2)}) collective-permute-start(f32[8,1]{0,1:T(1,128)S(1)} %convolution_bitcast_fusion), channel_id=1, source_target_pairs={{0,4},{4,0},{1,5},{5,1},{2,6},{6,2},{3,7},{7,3},{8,12},{12,8},{9,1... | collective-permute-start | bytes 104 | tf_op jit(solution)/shard_map/ppermute | solution.py:110
  56.4 7.5 %collective-permute-start.4 = (bf16[96,1,4,1,128]{4,0,3,2,1:T(8,128)(2,1)S(1)}, bf16[96,1,4,1,128]{4,0,3,2,1:T(8,128)(2,1)S(1)}, u32[]{:S(2)}, u32[]{:S(2)}) collective-permute-start(bf16[96,1,4,1,128]{4,0,3,2,1:T(8,128)(2,1)S(1)} %get-tuple-element.61), channel_id=1, source_target_pairs={{0,4},{1,5},{2,6},{3,7},{8,12},{9,13},{10,14},{11,15},{16,20},{17,... | collective-permute-start | bytes 294920 | tf_op jit(solution)/shard_map/ppermute | solution.py:17
  59.8 6.5 %collective-permute-start.5 = (bf16[96,1,4,1,128]{4,0,3,2,1:T(8,128)(2,1)S(1)}, bf16[96,1,4,1,128]{4,0,3,2,1:T(8,128)(2,1)S(1)}, u32[]{:S(2)}, u32[]{:S(2)}) collective-permute-start(bf16[96,1,4,1,128]{4,0,3,2,1:T(8,128)(2,1)S(1)} %get-tuple-element.62), channel_id=1, source_target_pairs={{4,0},{5,1},{6,2},{7,3},{12,8},{13,9},{14,10},{15,11},{20,16},{21,... | collective-permute-start | bytes 294920 | tf_op jit(solution)/shard_map/ppermute | solution.py:18
  68.1 1.2 copy-start.2
  69.1 1.5 copy-start.5
  69.1 2.7 %copy-start.7 = (bf16[864,1,4,2,128]{4,0,3,2,1:T(8,128)(2,1)}, bf16[864,1,4,2,128]{4,0,3,2,1:T(8,128)(2,1)S(1)}, u32[]{:S(2)}) copy-start(bf16[864,1,4,2,128]{4,0,3,2,1:T(8,128)(2,1)S(1)} %get-tuple-element.7) | copy-start | bytes 5308420
  69.3 2.5 %copy-start.3 = (bf16[864,1,4,2,128]{4,0,3,2,1:T(8,128)(2,1)}, bf16[864,1,4,2,128]{4,0,3,2,1:T(8,128)(2,1)S(1)}, u32[]{:S(2)}) copy-start(bf16[864,1,4,2,128]{4,0,3,2,1:T(8,128)(2,1)S(1)} %slice_dynamic-update-slice_fusion) | copy-start | bytes 5308420
  75.7 1.5 copy-start.6
  77.2 1.5 copy-start.4
  80.0 1.9 %copy-start.1 = (f32[2624,384]{1,0:T(8,128)}, f32[2624,384]{1,0:T(8,128)S(1)}, u32[]{:S(2)}) copy-start(f32[2624,384]{1,0:T(8,128)S(1)} %pad.10) | copy-start | bytes 12091396
  82.1 2.8 %collective-permute-start.6 = (bf16[1312,384]{1,0:T(8,128)(2,1)S(1)}, bf16[1312,384]{1,0:T(8,128)(2,1)}, u32[]{:S(2)}, u32[]{:S(2)}) collective-permute-start(bf16[1312,384]{1,0:T(8,128)(2,1)S(1)} %fusion.47), channel_id=1, source_target_pairs={{0,1},{1,0},{2,3},{3,2},{4,5},{5,4},{6,7},{7,6},{8,9},{9,8},{10,11... | collective-permute-start | bytes 3022856 | tf_op jit(solution)/shard_map/ppermute | solution.py:92
  87.8 13.8 %collective-permute-start.7 = (bf16[656,384]{1,0:T(8,128)(2,1)}, bf16[656,384]{1,0:T(8,128)(2,1)}, u32[]{:S(2)}, u32[]{:S(2)}) collective-permute-start(bf16[656,384]{1,0:T(8,128)(2,1)} %fusion.53), channel_id=1, source_target_pairs={{0,2},{1,3},{2,0},{3,1},{4,6},{5,7},{6,4},{7,5},{8,10},{9,11},{10,... | collective-permute-start | bytes 1511432 | tf_op jit(solution)/shard_map/ppermute | solution.py:92
  104.8 7.3 %collective-permute-start.8 = (bf16[328,384]{1,0:T(8,128)(2,1)S(1)}, bf16[328,384]{1,0:T(8,128)(2,1)S(1)}, u32[]{:S(2)}, u32[]{:S(2)}) collective-permute-start(bf16[328,384]{1,0:T(8,128)(2,1)S(1)} %fusion.86), channel_id=1, source_target_pairs={{0,4},{4,0},{1,5},{5,1},{2,6},{6,2},{3,7},{7,3},{8,12},{12,8},{9,1... | collective-permute-start | bytes 755720 | tf_op jit(solution)/shard_map/ppermute | solution.py:92
  113.2 6.5 %collective-permute-start.9 = (bf16[328,384]{1,0:T(8,128)(2,1)S(1)}, bf16[328,384]{1,0:T(8,128)(2,1)S(1)}, u32[]{:S(2)}, u32[]{:S(2)}) collective-permute-start(bf16[328,384]{1,0:T(8,128)(2,1)S(1)} %fusion.58), channel_id=1, source_target_pairs={{0,4},{4,0},{1,5},{5,1},{2,6},{6,2},{3,7},{7,3},{8,12},{12,8},{9,1... | collective-permute-start | bytes 755720 | tf_op jit(solution)/shard_map/ppermute | solution.py:98
  120.9 11.3 %collective-permute-start.10 = (bf16[656,384]{1,0:T(8,128)(2,1)}, bf16[656,384]{1,0:T(8,128)(2,1)}, u32[]{:S(2)}, u32[]{:S(2)}) collective-permute-start(bf16[656,384]{1,0:T(8,128)(2,1)} %get-tuple-element.57), channel_id=1, source_target_pairs={{0,2},{1,3},{2,0},{3,1},{4,6},{5,7},{6,4},{7,5},{8,10},{9,11},{10,... | collective-permute-start | bytes 1511432 | tf_op jit(solution)/shard_map/ppermute | solution.py:98
  122.9 9.3 %copy-start.8 = (bf16[1,656,384]{2,1,0:T(8,128)(2,1)S(1)}, bf16[1,656,384]{2,1,0:T(8,128)(2,1)}, u32[]{:S(2)}) copy-start(bf16[1,656,384]{2,1,0:T(8,128)(2,1)} %get-tuple-element.58) | copy-start | bytes 1511428
  123.9 22.6 %all-to-all-start.2 = ((bf16[4,96,1,4,2,128]{5,1,4,3,2,0:T(8,128)(2,1)}), bf16[4,96,1,4,2,128]{5,1,4,3,2,0:T(8,128)(2,1)S(1)}, u32[]{:S(2)}, u32[]{:S(2)}) async-start(bf16[4,96,1,4,2,128]{5,1,4,3,2,0:T(8,128)(2,1)} %copy.32), calls=%async_computation.2 | async-start | bytes 1572864 | tf_op jit(solution)/shard_map/all_to_all | solution.py:185
  133.7 12.9 %copy-start.13 = (f32[96]{0:T(128)S(1)}, f32[96]{0:T(128)}, u32[]{:S(2)}) copy-start(f32[96]{0:T(128)} %param.24) | copy-start | bytes 1156
  134.8 12.8 %collective-permute-start.11 = (bf16[1312,384]{1,0:T(8,128)(2,1)}, bf16[1312,384]{1,0:T(8,128)(2,1)}, u32[]{:S(2)}, u32[]{:S(2)}) collective-permute-start(bf16[1312,384]{1,0:T(8,128)(2,1)} %get-tuple-element.53), channel_id=1, source_target_pairs={{0,1},{1,0},{2,3},{3,2},{4,5},{5,4},{6,7},{7,6},{8,9},{9,8},{10,11... | collective-permute-start | bytes 3022856 | tf_op jit(solution)/shard_map/ppermute | solution.py:98
where the time goes:
time: 153 us; the launch traced here: 152 us
  waiting for transfers between devices  62.7 us (41%)
  starting transfers between devices  30.6 us (20%)
  other arithmetic  19.2 us (13%)
  local copies, waits for them, and re-layouts  16.6 us (11%)
  matrix products  12.6 us (8%)
  blocking collectives  8.66 us (6%)
  between operations  1.87 us (1%)
    ppermute x3, waiting for transfers between devices, butterfly_sum(): got = lax.ppermute(send.astype(jnp.bfloat16), axis, perm)  22.1 us
    all_to_all x1, waiting for transfers between devices, body(): parts = lax.all_to_all(parts, 'ch', split_axis=0, concat_axis=0, tiled=True)  11.7 us
    ppermute x3, waiting for transfers between devices, butterfly_sum(): got = lax.ppermute(work, axis, perm)  9.43 us
    all_gather x1, blocking collectives, body(): piece = lax.all_gather(pairs, 'ha', axis=1, tiled=True)  8.66 us
    unnamed x39, local copies, waits for them, and re-layouts  5.97 us
    all_to_all x1, waiting for transfers between devices, body(): lax.all_to_all(projected, 'ch', split_axis=0, concat_axis=2, tiled=True)  5.88 us
    ppermute x4, waiting for transfers between devices, doubling_sum(): got = lax.ppermute(values, axis, perm)  5.65 us
    all_to_all x1, waiting for transfers between devices, body(): lax.all_to_all(normed, 'ch', split_axis=2, concat_axis=0, tiled=True)  5.55 us
  transfers between devices with their start and end apart: 16, of which 13 were waited for; matrix products, arithmetic and copies ran while one was open for 11% of the time, Pallas kernels for 0%

commit v1 on v0

--- a/solution.py
+++ b/solution.py
@@ -5,6 +5,17 @@
 
 GROUPS = 32
 EPS = 1e-06
+
+
+def axis_part_save(my_data, ndim_at, array_in):
+    side_arr, e_next = (my_data.shape[:ndim_at], my_data.shape[ndim_at + 1 :])
+    return jnp.moveaxis(my_data.reshape(*side_arr, array_in, -1, *e_next), ndim_at, 0)
+
+
+def _perform_columns(base_x, dim_at):
+    base_x = jnp.moveaxis(base_x, 0, dim_at)
+    x_now = base_x.shape
+    return base_x.reshape(*x_now[:dim_at], x_now[dim_at] * x_now[dim_at + 1], *x_now[dim_at + 2 :])
 
 
 def padded_2(x, sides, width):
@@ -192,7 +203,14 @@
     full_width = chans * lax.axis_size("ch")
     carry = jnp.zeros((3, 9 * chans, full_width), jnp.float32)
     copies = jnp.broadcast_to(masked_cot[None], (shares,) + masked_cot.shape)
-    piece = lax.all_to_all(copies, "ch", split_axis=0, concat_axis=0, tiled=True)
+    shaped, all_rows = (lax.axis_size("ch"), lax.axis_index("ch"))
+    now = axis_part_save(copies, 0, shaped)
+    store = [now[all_rows]]
+    for pp in range(1, shaped):
+        spare = now[all_rows ^ pp]
+        store.append(lax.ppermute(spare, "ch", [(d, d ^ pp) for d in range(shaped)]))
+    now = jnp.stack(store, 0)[all_rows ^ jnp.arange(shaped)]
+    piece = _perform_columns(now, 0)
     piece = piece.reshape((shares * chans,) + masked_cot.shape[1:])
     start = jnp.int32(0)
     for time_tap in range(3):

time: 153 us -> 149 us (0.974)
  waiting for transfers between devices: 62.7 us -> 51.9 us
  starting transfers between devices: 30.6 us -> 36.4 us
  other arithmetic: 19.2 us -> 22.9 us
  matrix products: 12.6 us -> 9.13 us
    all_to_all x1, waiting for transfers between devices: 5.55 us -> 0.01 us  [body(): lax.all_to_all(normed, 'ch', split_axis=2, concat_axis=0, tiled=True)]
    ppermute x0 -> x3, starting transfers between devices: none -> 4.39 us  [body(): lax.ppermute(spare, 'ch', [(d, d ^ pp) for d in range(shaped)])]
    all_to_all x1 -> x0, starting transfers between devices: 3.49 us -> none  [body(): lax.all_to_all(copies, 'ch', split_axis=0, concat_axis=0, tiled=True)]
    ppermute x3, starting transfers between devices: 1.84 us -> 4.91 us  [butterfly_sum(): got = lax.ppermute(send.astype(jnp.bfloat16), axis, perm)]
    gather x0 -> x1, local copies, waits for them, and re-layouts: none -> 2.96 us  [body(): now = jnp.stack(store, 0)[all_rows ^ jnp.arange(shaped)]]
    another operation x0 -> x1, other arithmetic: none -> 2.68 us  [body(): now = jnp.stack(store, 0)[all_rows ^ jnp.arange(shaped)]]
    ppermute x1, waiting for transfers between devices: 2.46 us -> 0.01 us  [padded_2(): after = lax.ppermute(leading, axis, down)]
    squeeze x3, other arithmetic: 3.7 us -> 1.45 us  [butterfly_sum(): first = lax.dynamic_index_in_dim(pair, side, keepdims=False)]
  transfers between devices with their start and end apart: 16 -> 18, of which waited for: 13 -> 11; matrix products, arithmetic and copies ran while one was open for 11% -> 13% of each run, Pallas kernels for 0% -> 0%
where the time goes in v1:
time: 149 us; the launch traced here: 148 us
  waiting for transfers between devices  51.9 us (35%)
  starting transfers between devices  36.4 us (24%)
  other arithmetic  22.9 us (15%)
  local copies, waits for them, and re-layouts  16.6 us (11%)
  matrix products  9.13 us (6%)
  blocking collectives  8.97 us (6%)
  between operations  1.84 us (1%)
    ppermute x3, waiting for transfers between devices, butterfly_sum(): got = lax.ppermute(send.astype(jnp.bfloat16), axis, perm)  20.6 us
    all_to_all x1, waiting for transfers between devices, body(): parts = lax.all_to_all(parts, 'ch', split_axis=0, concat_axis=0, tiled=True)  11.5 us
    ppermute x3, waiting for transfers between devices, butterfly_sum(): got = lax.ppermute(work, axis, perm)  9.8 us
    all_gather x1, blocking collectives, body(): piece = lax.all_gather(pairs, 'ha', axis=1, tiled=True)  8.97 us
    ppermute x4, waiting for transfers between devices, doubling_sum(): got = lax.ppermute(values, axis, perm)  5.63 us
    unnamed x29, local copies, waits for them, and re-layouts  5.28 us
    ppermute x4, starting transfers between devices, doubling_sum(): got = lax.ppermute(values, axis, perm)  5.03 us
    ppermute x3, starting transfers between devices, butterfly_sum(): got = lax.ppermute(send.astype(jnp.bfloat16), axis, perm)  4.91 us
  transfers between devices with their start and end apart: 18, of which 11 were waited for; matrix products, arithmetic and copies ran while one was open for 13% of the time, Pallas kernels for 0%

profile of v1, /device:TPU:0, one launch (start us, length us, event | category | flops | bytes accessed | tf_op | source)
XLA Modules:
  0.0 147.8 jit_solution(7012015875894893071)
XLA Ops:
  1.4 1.1 fusion.68
  2.8 3.0 %collective-permute-start = (f32[8,1]{0,1:T(1,128)S(1)}, f32[8,1]{0,1:T(1,128)S(1)}, u32[]{:S(2)}, u32[]{:S(2)}) collective-permute-start(f32[8,1]{0,1:T(1,128)S(1)} %convolution_bitcast_fusion.3), channel_id=1, source_target_pairs={{0,4},{4,0},{1,5},{5,1},{2,6},{6,2},{3,7},{7,3},{8,12},{12,8},{9,1... | collective-permute-start | bytes 104 | tf_op jit(solution)/shard_map/ppermute | solution.py:121
  6.1 1.2 collective-permute-done
  7.4 2.3 %collective-permute-done.1 = f32[8,1]{0,1:T(1,128)S(1)} collective-permute-done((f32[8,1]{0,1:T(1,128)S(1)}, f32[8,1]{0,1:T(1,128)S(1)}, u32[]{:S(2)}, u32[]{:S(2)}) %collective-permute-start.1) | collective-permute-done | bytes 64 | tf_op jit(solution)/shard_map/ppermute | solution.py:121
  10.0 1.8 %fusion.94 = bf16[96,1,4,2,128]{4,0,3,1,2:T(8,128)(2,1)} fusion(f32[96]{0:T(128)} %param.16, f32[96]{0:T(128)} %param.15, f32[96]{0:T(128)S(1)} %mul.117, f32[96]{0:T(128)S(1)} %sub.78, bf16[96,1,4,2,128]{4,3,2,1,0:T(2,128)(2,1)} %param.13), kind=kLoop, calls=%fused_computation.124 | loop fusion | flops 589824 | bytes 394752 | tf_op jit(solution)/shard_map/convert_element_type | solution.py:147
  11.8 4.9 %all-to-all-start = ((bf16[96,1,4,2,128]{4,0,3,1,2:T(8,128)(2,1)}), bf16[96,1,4,2,128]{4,0,3,1,2:T(8,128)(2,1)S(1)}, u32[]{:S(2)}, u32[]{:S(2)}) async-start(bf16[96,1,4,2,128]{4,0,3,1,2:T(8,128)(2,1)} %fusion.94), calls=%async_computation | async-start | bytes 393216 | tf_op jit(solution)/shard_map/all_to_all | solution.py:150
  16.7 2.0 %multiply_bitcast_fusion.1 = (bf16[1,1,96,1,4,2,128]{6,5,4,2,3,1,0:T(2,128)(2,1)}, bf16[1,96,1,4,2,128]{5,4,3,1,2,0:T(2,128)(2,1)}) fusion(bf16[96,1,4,2,128]{4,3,2,1,0:T(2,128)(2,1)} %param.25, bf16[4]{0:T(256)(128)(2,1)S(1)} %fusion.116), kind=kLoop, calls=%fused_computation.161 | loop fusion | flops 98304 | bytes 589832 | tf_op jit(solution)/shard_map/reshape | solution.py:12
  18.6 2.0 %collective-permute-start.6 = (bf16[1,96,1,4,2,128]{5,4,3,1,2,0:T(2,128)(2,1)}, bf16[1,96,1,4,2,128]{5,4,3,1,2,0:T(2,128)(2,1)}, u32[]{:S(2)}, u32[]{:S(2)}) collective-permute-start(bf16[1,96,1,4,2,128]{5,4,3,1,2,0:T(2,128)(2,1)} %get-tuple-element.62), channel_id=1, source_target_pairs={{0,8},{8,0},{16,24},{24,16},{1,9},{9,1},{17,25},{25,17},{2,10},{10... | collective-permute-start | bytes 589832 | tf_op jit(solution)/shard_map/ppermute | solution.py:211
  20.7 2.4 %collective-permute-start.7 = (bf16[1,96,1,4,2,128]{5,4,3,1,2,0:T(2,128)(2,1)}, bf16[1,96,1,4,2,128]{5,4,3,1,2,0:T(2,128)(2,1)}, u32[]{:S(2)}, u32[]{:S(2)}) collective-permute-start(bf16[1,96,1,4,2,128]{5,4,3,1,2,0:T(2,128)(2,1)} %get-tuple-element.62), channel_id=1, source_target_pairs={{0,16},{8,24},{16,0},{24,8},{1,17},{9,25},{17,1},{25,9},{2,18},{10... | collective-permute-start | bytes 589832 | tf_op jit(solution)/shard_map/ppermute | solution.py:211
  23.0 0.7 slice.123
  23.9 0.4 fusion.37
  24.3 9.0 %all-gather = bf16[512,768]{1,0:T(8,128)(2,1)S(1)} all-gather(bf16[256,768]{1,0:T(8,128)(2,1)S(1)} %fusion.37), channel_id=2, replica_groups=mesh['ch'=4,'ha'=2,'dp'=4] {'ha'}, dimensions={0}, use_global_device_ids=true | all-gather | bytes 1179648 | tf_op jit(solution)/shard_map/all_gather | solution.py:169
  33.3 0.6 fusion.123
  34.2 0.6 fusion.46
  34.8 0.9 copy.32
  35.6 4.8 %all-to-all-start.1 = ((bf16[384,1,1,2,128]{4,3,2,1,0:T(2,128)(2,1)}), bf16[384,1,1,2,128]{4,3,2,1,0:T(2,128)(2,1)S(1)}, u32[]{:S(2)}, u32[]{:S(2)}) async-start(bf16[384,1,1,2,128]{4,3,2,1,0:T(2,128)(2,1)} %copy.32), calls=%async_computation.1 | async-start | bytes 393216 | tf_op jit(solution)/shard_map/all_to_all | solution.py:176
  40.5 1.8 %fusion.121 = (bf16[1,3,3,96,384]{4,3,2,1,0:T(8,128)(2,1)S(1)}, bf16[1,3,3,96,384]{4,3,2,1,0:T(8,128)(2,1)S(1)}, bf16[1,3,3,96,384]{4,3,2,1,0:T(8,128)(2,1)S(1)}) fusion(bf16[3,3,3,96,384]{4,3,2,1,0:T(8,128)(2,1)} %param.23), kind=kLoop, calls=%fused_computation.187 | loop fusion | bytes 3981312 | tf_op jit(solution)/shard_map/slice | solution.py:189
  42.3 4.4 %all-to-all-done.1 = bf16[384,1,1,2,128]{4,3,2,1,0:T(2,128)(2,1)S(1)} async-done(((bf16[384,1,1,2,128]{4,3,2,1,0:T(2,128)(2,1)}), bf16[384,1,1,2,128]{4,3,2,1,0:T(2,128)(2,1)S(1)}, u32[]{:S(2)}, u32[]{:S(2)}) %all-to-all-start.1) | async-done | bytes 196640 | tf_op jit(solution)/shard_map/all_to_all | solution.py:176
  47.3 0.5 collective-permute-start.2
  48.1 1.5 %collective-permute-start.3 = (f32[8,1]{0,1:T(1,128)S(1)}, f32[8,1]{0,1:T(1,128)S(1)}, u32[]{:S(2)}, u32[]{:S(2)}) collective-permute-start(f32[8,1]{0,1:T(1,128)S(1)} %convolution_bitcast_fusion), channel_id=1, source_target_pairs={{0,4},{4,0},{1,5},{5,1},{2,6},{6,2},{3,7},{7,3},{8,12},{12,8},{9,1... | collective-permute-start | bytes 104 | tf_op jit(solution)/shard_map/ppermute | solution.py:121
  49.6 1.2 collective-permute-done.2
  50.8 0.8 collective-permute-done.3
  52.0 0.3 fusion.78
  52.3 0.7 fusion.122
  53.0 4.0 %collective-permute-start.4 = (bf16[96,1,4,1,128]{4,0,3,2,1:T(8,128)(2,1)}, bf16[96,1,4,1,128]{4,0,3,2,1:T(8,128)(2,1)}, u32[]{:S(2)}, u32[]{:S(2)}) collective-permute-start(bf16[96,1,4,1,128]{4,0,3,2,1:T(8,128)(2,1)} %get-tuple-element.63), channel_id=1, source_target_pairs={{0,4},{1,5},{2,6},{3,7},{8,12},{9,13},{10,14},{11,15},{16,20},{17,... | collective-permute-start | bytes 294920 | tf_op jit(solution)/shard_map/ppermute | solution.py:28
  57.1 1.3 collective-permute-start.5
  58.4 2.7 %maximum_bitcast_fusion = bf16[4,96,4,2,128]{4,3,2,1,0:T(2,128)(2,1)S(1)} fusion(bf16[1,1,96,1,4,2,128]{6,5,4,2,3,1,0:T(2,128)(2,1)} %bitcast.50, bf16[1,1,96,1,4,2,128]{6,5,4,2,3,1,0:T(2,128)(2,1)} %bitcast.49, bf16[1,1,96,1,4,2,128]{6,5,4,2,3,1,0:T(2,128)(2,1)} %bitcast.48, bf16[1,1,96,1,4,2,128]{6,5,4,2,3,1,0:T(2,128)(2,1)} %get-tuple-element.61), kind=kLoop, calls=%fused_computation.67 | loop fusion | flops 1179648 | bytes 1572864 | tf_op jit(solution)/shard_map/stack | solution.py:212
  61.1 3.0 %gather_fusion = bf16[4,96,4,2,128]{4,3,2,1,0:T(2,128)(2,1)} fusion(bf16[4,96,4,2,128]{4,3,2,1,0:T(2,128)(2,1)S(1)} %maximum_bitcast_fusion, s32[1024]{0:T(1024)S(1)} %pad_clamp_fusion), kind=kCustom, calls=%fused_computation | custom fusion | bytes 1572880 | tf_op jit(solution)/shard_map/gather | solution.py:212
  64.0 1.3 fusion.41
  66.2 0.9 fusion.99
  67.2 0.3 slice_dynamic-update-slice_fusion.9
  67.6 0.4 constant_dynamic-update-slice_fusion
  68.6 0.9 fusion.98
  69.7 1.2 fusion.13
  70.9 1.2 fusion.15
  72.2 1.3 fusion.34
  73.4 1.1 fusion.19
  74.8 1.1 fusion.25
  75.9 1.1 fusion.31
  77.3 1.9 %copy-done.1 = f32[2624,384]{1,0:T(8,128)} copy-done((f32[2624,384]{1,0:T(8,128)}, f32[2624,384]{1,0:T(8,128)S(1)}, u32[]{:S(2)}) %copy-start.1) | copy-done | bytes 4030488
  79.4 2.7 %collective-permute-done.9 = bf16[1312,384]{1,0:T(8,128)(2,1)} collective-permute-done((bf16[1312,384]{1,0:T(8,128)(2,1)S(1)}, bf16[1312,384]{1,0:T(8,128)(2,1)}, u32[]{:S(2)}, u32[]{:S(2)}) %collective-permute-start.9) | collective-permute-done | bytes 1007648 | tf_op jit(solution)/shard_map/ppermute | solution.py:103
  82.1 2.0 %bitcast_add_fusion = f32[1312,384]{1,0:T(8,128)S(1)} fusion(bf16[1312,384]{1,0:T(8,128)(2,1)} %collective-permute-done.9, f32[2,1312,384]{2,1,0:T(8,128)} %bitcast.220, s32[]{:T(128)S(6)} %select_n.45), kind=kLoop, calls=%fused_computation.13 | loop fusion | flops 1007616 | bytes 5038084 | tf_op jit(solution)/shard_map/add | solution.py:104
  84.1 0.8 fusion.56
  85.0 1.5 %collective-permute-start.10 = (bf16[656,384]{1,0:T(8,128)(2,1)}, bf16[656,384]{1,0:T(8,128)(2,1)}, u32[]{:S(2)}, u32[]{:S(2)}) collective-permute-start(bf16[656,384]{1,0:T(8,128)(2,1)} %fusion.56), channel_id=1, source_target_pairs={{0,2},{1,3},{2,0},{3,1},{4,6},{5,7},{6,4},{7,5},{8,10},{9,11},{10,... | collective-permute-start | bytes 1511432 | tf_op jit(solution)/shard_map/ppermute | solution.py:103
  86.5 12.3 %collective-permute-done.10 = bf16[656,384]{1,0:T(8,128)(2,1)} collective-permute-done((bf16[656,384]{1,0:T(8,128)(2,1)}, bf16[656,384]{1,0:T(8,128)(2,1)}, u32[]{:S(2)}, u32[]{:S(2)}) %collective-permute-start.10) | collective-permute-done | bytes 503840 | tf_op jit(solution)/shard_map/ppermute | solution.py:103
  98.8 1.1 bitcast_add_fusion.1
  100.0 0.9 copy-done.2
  100.9 3.3 %collective-permute-start.11 = (bf16[328,384]{1,0:T(8,128)(2,1)S(1)}, bf16[328,384]{1,0:T(8,128)(2,1)S(1)}, u32[]{:S(2)}, u32[]{:S(2)}) collective-permute-start(bf16[328,384]{1,0:T(8,128)(2,1)S(1)} %fusion.89), channel_id=1, source_target_pairs={{0,4},{4,0},{1,5},{5,1},{2,6},{6,2},{3,7},{7,3},{8,12},{12,8},{9,1... | collective-permute-start | bytes 755720 | tf_op jit(solution)/shard_map/ppermute | solution.py:103
  104.3 5.5 %collective-permute-done.11 = bf16[328,384]{1,0:T(8,128)(2,1)S(1)} collective-permute-done((bf16[328,384]{1,0:T(8,128)(2,1)S(1)}, bf16[328,384]{1,0:T(8,128)(2,1)S(1)}, u32[]{:S(2)}, u32[]{:S(2)}) %collective-permute-start.11) | collective-permute-done | bytes 251936 | tf_op jit(solution)/shard_map/ppermute | solution.py:103
  109.8 1.1 fusion.61
  110.9 1.8 %collective-permute-start.12 = (bf16[328,384]{1,0:T(8,128)(2,1)S(1)}, bf16[328,384]{1,0:T(8,128)(2,1)S(1)}, u32[]{:S(2)}, u32[]{:S(2)}) collective-permute-start(bf16[328,384]{1,0:T(8,128)(2,1)S(1)} %fusion.61), channel_id=1, source_target_pairs={{0,4},{4,0},{1,5},{5,1},{2,6},{6,2},{3,7},{7,3},{8,12},{12,8},{9,1... | collective-permute-start | bytes 755720 | tf_op jit(solution)/shard_map/ppermute | solution.py:109
  112.7 5.0 %collective-permute-done.12 = bf16[328,384]{1,0:T(8,128)(2,1)S(1)} collective-permute-done((bf16[328,384]{1,0:T(8,128)(2,1)S(1)}, bf16[328,384]{1,0:T(8,128)(2,1)S(1)}, u32[]{:S(2)}, u32[]{:S(2)}) %collective-permute-start.12) | collective-permute-done | bytes 251936 | tf_op jit(solution)/shard_map/ppermute | solution.py:109
  117.9 0.9 pad_maximum_fusion.2
  118.7 1.5 %collective-permute-start.13 = (bf16[656,384]{1,0:T(8,128)(2,1)}, bf16[656,384]{1,0:T(8,128)(2,1)S(1)}, u32[]{:S(2)}, u32[]{:S(2)}) collective-permute-start(bf16[656,384]{1,0:T(8,128)(2,1)} %get-tuple-element.57), channel_id=1, source_target_pairs={{0,2},{1,3},{2,0},{3,1},{4,6},{5,7},{6,4},{7,5},{8,10},{9,11},{10,... | collective-permute-start | bytes 1511432 | tf_op jit(solution)/shard_map/ppermute | solution.py:109
  120.3 0.4 copy.35
  120.6 1.0 copy.36
  121.6 3.7 %all-to-all-start.2 = ((bf16[4,96,1,4,2,128]{5,1,4,3,2,0:T(8,128)(2,1)}), bf16[4,96,1,4,2,128]{5,1,4,3,2,0:T(8,128)(2,1)S(1)}, u32[]{:S(2)}, u32[]{:S(2)}) async-start(bf16[4,96,1,4,2,128]{5,1,4,3,2,0:T(8,128)(2,1)} %copy.36), calls=%async_computation.2 | async-start | bytes 1572864 | tf_op jit(solution)/shard_map/all_to_all | solution.py:196
  125.3 4.8 %collective-permute-done.13 = bf16[656,384]{1,0:T(8,128)(2,1)S(1)} collective-permute-done((bf16[656,384]{1,0:T(8,128)(2,1)}, bf16[656,384]{1,0:T(8,128)(2,1)S(1)}, u32[]{:S(2)}, u32[]{:S(2)}) %collective-permute-start.13) | collective-permute-done | bytes 503840 | tf_op jit(solution)/shard_map/ppermute | solution.py:109
  130.2 0.4 fusion.60
  130.6 1.1 pad_maximum_fusion.1
  131.7 11.5 %all-to-all-done.2 = bf16[4,96,1,4,2,128]{5,1,4,3,2,0:T(8,128)(2,1)S(1)} async-done(((bf16[4,96,1,4,2,128]{5,1,4,3,2,0:T(8,128)(2,1)}), bf16[4,96,1,4,2,128]{5,1,4,3,2,0:T(8,128)(2,1)S(1)}, u32[]{:S(2)}, u32[]{:S(2)}) %all-to-all-start.2) | async-done | bytes 786464 | tf_op jit(solution)/shard_map/all_to_all | solution.py:196
  143.5 0.8 copy.40
  144.3 0.8 fusion.51
  145.3 2.4 %convert.5 = f32[3,3,3,96,384]{4,3,2,1,0:T(8,128)} convert(bf16[3,3,3,96,384]{4,3,2,1,0:T(8,128)(2,1)S(1)} %bitcast.221) | non-fusion elementwise | flops 995328 | bytes 5971968 | tf_op jit(solution)/shard_map/reshape | solution.py:227
  (79 shorter events, 5.6 us)
Async XLA Ops:
  0.6 33.6 %copy-start = (bf16[384,384]{1,0:T(8,128)(2,1)S(1)}, bf16[384,384]{1,0:T(8,128)(2,1)}, u32[]{:S(2)}) copy-start(bf16[384,384]{1,0:T(8,128)(2,1)} %param.19) | copy-start | bytes 884740
  0.6 23.3 %copy-start.8 = (bf16[384,1152]{1,0:T(8,128)(2,1)S(1)}, bf16[384,1152]{1,0:T(8,128)(2,1)}, u32[]{:S(2)}) copy-start(bf16[384,1152]{1,0:T(8,128)(2,1)} %param.17) | copy-start | bytes 2654212
  2.8 4.5 %collective-permute-start = (f32[8,1]{0,1:T(1,128)S(1)}, f32[8,1]{0,1:T(1,128)S(1)}, u32[]{:S(2)}, u32[]{:S(2)}) collective-permute-start(f32[8,1]{0,1:T(1,128)S(1)} %convolution_bitcast_fusion.3), channel_id=1, source_target_pairs={{0,4},{4,0},{1,5},{5,1},{2,6},{6,2},{3,7},{7,3},{8,12},{12,8},{9,1... | collective-permute-start | bytes 104 | tf_op jit(solution)/shard_map/ppermute | solution.py:121
  6.1 3.6 %collective-permute-start.1 = (f32[8,1]{0,1:T(1,128)S(1)}, f32[8,1]{0,1:T(1,128)S(1)}, u32[]{:S(2)}, u32[]{:S(2)}) collective-permute-start(f32[8,1]{0,1:T(1,128)S(1)} %convolution_bitcast_fusion.2), channel_id=1, source_target_pairs={{0,4},{4,0},{1,5},{5,1},{2,6},{6,2},{3,7},{7,3},{8,12},{12,8},{9,1... | collective-permute-start | bytes 104 | tf_op jit(solution)/shard_map/ppermute | solution.py:121
  11.8 11.9 %all-to-all-start = ((bf16[96,1,4,2,128]{4,0,3,1,2:T(8,128)(2,1)}), bf16[96,1,4,2,128]{4,0,3,1,2:T(8,128)(2,1)S(1)}, u32[]{:S(2)}, u32[]{:S(2)}) async-start(bf16[96,1,4,2,128]{4,0,3,1,2:T(8,128)(2,1)} %fusion.94), calls=%async_computation | async-start | bytes 393216 | tf_op jit(solution)/shard_map/all_to_all | solution.py:150
  16.7 16.6 %slice-start = ((f32[1152]{0:T(1024)}), f32[384]{0:T(512)S(1)}, s32[]{:S(2)}) async-start(f32[1152]{0:T(1024)} %param.18), calls=%async_computation.3 | async-start | bytes 4096 | tf_op jit(solution)/shard_map/slice | solution.py:158
  18.6 39.7 %collective-permute-start.6 = (bf16[1,96,1,4,2,128]{5,4,3,1,2,0:T(2,128)(2,1)}, bf16[1,96,1,4,2,128]{5,4,3,1,2,0:T(2,128)(2,1)}, u32[]{:S(2)}, u32[]{:S(2)}) collective-permute-start(bf16[1,96,1,4,2,128]{5,4,3,1,2,0:T(2,128)(2,1)} %get-tuple-element.62), channel_id=1, source_target_pairs={{0,8},{8,0},{16,24},{24,16},{1,9},{9,1},{17,25},{25,17},{2,10},{10... | collective-permute-start | bytes 589832 | tf_op jit(solution)/shard_map/ppermute | solution.py:211
  20.7 37.7 %collective-permute-start.7 = (bf16[1,96,1,4,2,128]{5,4,3,1,2,0:T(2,128)(2,1)}, bf16[1,96,1,4,2,128]{5,4,3,1,2,0:T(2,128)(2,1)}, u32[]{:S(2)}, u32[]{:S(2)}) collective-permute-start(bf16[1,96,1,4,2,128]{5,4,3,1,2,0:T(2,128)(2,1)} %get-tuple-element.62), channel_id=1, source_target_pairs={{0,16},{8,24},{16,0},{24,8},{1,17},{9,25},{17,1},{25,9},{2,18},{10... | collective-permute-start | bytes 589832 | tf_op jit(solution)/shard_map/ppermute | solution.py:211
  23.0 35.3 %collective-permute-start.8 = (bf16[1,96,1,4,2,128]{5,4,3,1,2,0:T(2,128)(2,1)}, bf16[1,96,1,4,2,128]{5,4,3,1,2,0:T(2,128)(2,1)}, u32[]{:S(2)}, u32[]{:S(2)}) collective-permute-start(bf16[1,96,1,4,2,128]{5,4,3,1,2,0:T(2,128)(2,1)} %get-tuple-element.62), channel_id=1, source_target_pairs={{0,24},{8,16},{16,8},{24,0},{1,25},{9,17},{17,9},{25,1},{2,26},{10... | collective-permute-start | bytes 589832 | tf_op jit(solution)/shard_map/ppermute | solution.py:211
  24.3 9.9 %copy-start.9 = (f32[384]{0:T(512)S(1)}, f32[384]{0:T(512)}, u32[]{:S(2)}) copy-start(f32[384]{0:T(512)} %param.20) | copy-start | bytes 4612
  35.6 11.1 %all-to-all-start.1 = ((bf16[384,1,1,2,128]{4,3,2,1,0:T(2,128)(2,1)}), bf16[384,1,1,2,128]{4,3,2,1,0:T(2,128)(2,1)S(1)}, u32[]{:S(2)}, u32[]{:S(2)}) async-start(bf16[384,1,1,2,128]{4,3,2,1,0:T(2,128)(2,1)} %copy.32), calls=%async_computation.1 | async-start | bytes 393216 | tf_op jit(solution)/shard_map/all_to_all | solution.py:176
  40.5 6.3 %copy-start.3 = (bf16[96,1,4,2,128]{4,3,2,1,0:T(2,128)(2,1)S(1)}, bf16[96,1,4,2,128]{4,3,2,1,0:T(2,128)(2,1)}, u32[]{:S(2)}) copy-start(bf16[96,1,4,2,128]{4,3,2,1,0:T(2,128)(2,1)} %param.13) | copy-start | bytes 589828
  40.5 11.5 %copy-start.5 = (f32[96]{0:T(128)S(1)}, f32[96]{0:T(128)}, u32[]{:S(2)}) copy-start(f32[96]{0:T(128)} %param.22) | copy-start | bytes 1156
  40.5 11.5 %copy-start.6 = (f32[96]{0:T(128)S(1)}, f32[96]{0:T(128)}, u32[]{:S(2)}) copy-start(f32[96]{0:T(128)} %param.21) | copy-start | bytes 1156
  47.3 3.6 %collective-permute-start.2 = (f32[8,1]{0,1:T(1,128)S(1)}, f32[8,1]{0,1:T(1,128)S(1)}, u32[]{:S(2)}, u32[]{:S(2)}) collective-permute-start(f32[8,1]{0,1:T(1,128)S(1)} %convolution_bitcast_fusion.1), channel_id=1, source_target_pairs={{0,4},{4,0},{1,5},{5,1},{2,6},{6,2},{3,7},{7,3},{8,12},{12,8},{9,1... | collective-permute-start | bytes 104 | tf_op jit(solution)/shard_map/ppermute | solution.py:121
  48.1 3.6 %collective-permute-start.3 = (f32[8,1]{0,1:T(1,128)S(1)}, f32[8,1]{0,1:T(1,128)S(1)}, u32[]{:S(2)}, u32[]{:S(2)}) collective-permute-start(f32[8,1]{0,1:T(1,128)S(1)} %convolution_bitcast_fusion), channel_id=1, source_target_pairs={{0,4},{4,0},{1,5},{5,1},{2,6},{6,2},{3,7},{7,3},{8,12},{12,8},{9,1... | collective-permute-start | bytes 104 | tf_op jit(solution)/shard_map/ppermute | solution.py:121
  53.0 11.0 %collective-permute-start.4 = (bf16[96,1,4,1,128]{4,0,3,2,1:T(8,128)(2,1)}, bf16[96,1,4,1,128]{4,0,3,2,1:T(8,128)(2,1)}, u32[]{:S(2)}, u32[]{:S(2)}) collective-permute-start(bf16[96,1,4,1,128]{4,0,3,2,1:T(8,128)(2,1)} %get-tuple-element.63), channel_id=1, source_target_pairs={{0,4},{1,5},{2,6},{3,7},{8,12},{9,13},{10,14},{11,15},{16,20},{17,... | collective-permute-start | bytes 294920 | tf_op jit(solution)/shard_map/ppermute | solution.py:28
  57.1 7.0 %collective-permute-start.5 = (bf16[96,1,4,1,128]{4,0,3,2,1:T(8,128)(2,1)}, bf16[96,1,4,1,128]{4,0,3,2,1:T(8,128)(2,1)}, u32[]{:S(2)}, u32[]{:S(2)}) collective-permute-start(bf16[96,1,4,1,128]{4,0,3,2,1:T(8,128)(2,1)} %get-tuple-element.64), channel_id=1, source_target_pairs={{4,0},{5,1},{6,2},{7,3},{12,8},{13,9},{14,10},{15,11},{20,16},{21,... | collective-permute-start | bytes 294920 | tf_op jit(solution)/shard_map/ppermute | solution.py:29
  72.1 1.3 copy-start.4
  77.3 1.9 %copy-start.1 = (f32[2624,384]{1,0:T(8,128)}, f32[2624,384]{1,0:T(8,128)S(1)}, u32[]{:S(2)}) copy-start(f32[2624,384]{1,0:T(8,128)S(1)} %pad.10) | copy-start | bytes 12091396
  79.3 2.8 %collective-permute-start.9 = (bf16[1312,384]{1,0:T(8,128)(2,1)S(1)}, bf16[1312,384]{1,0:T(8,128)(2,1)}, u32[]{:S(2)}, u32[]{:S(2)}) collective-permute-start(bf16[1312,384]{1,0:T(8,128)(2,1)S(1)} %fusion.47), channel_id=1, source_target_pairs={{0,1},{1,0},{2,3},{3,2},{4,5},{5,4},{6,7},{7,6},{8,9},{9,8},{10,11... | collective-permute-start | bytes 3022856 | tf_op jit(solution)/shard_map/ppermute | solution.py:103
  85.0 13.8 %collective-permute-start.10 = (bf16[656,384]{1,0:T(8,128)(2,1)}, bf16[656,384]{1,0:T(8,128)(2,1)}, u32[]{:S(2)}, u32[]{:S(2)}) collective-permute-start(bf16[656,384]{1,0:T(8,128)(2,1)} %fusion.56), channel_id=1, source_target_pairs={{0,2},{1,3},{2,0},{3,1},{4,6},{5,7},{6,4},{7,5},{8,10},{9,11},{10,... | collective-permute-start | bytes 1511432 | tf_op jit(solution)/shard_map/ppermute | solution.py:103
  100.0 1.0 copy-start.2
  100.9 8.8 %collective-permute-start.11 = (bf16[328,384]{1,0:T(8,128)(2,1)S(1)}, bf16[328,384]{1,0:T(8,128)(2,1)S(1)}, u32[]{:S(2)}, u32[]{:S(2)}) collective-permute-start(bf16[328,384]{1,0:T(8,128)(2,1)S(1)} %fusion.89), channel_id=1, source_target_pairs={{0,4},{4,0},{1,5},{5,1},{2,6},{6,2},{3,7},{7,3},{8,12},{12,8},{9,1... | collective-permute-start | bytes 755720 | tf_op jit(solution)/shard_map/ppermute | solution.py:103
  110.9 6.8 %collective-permute-start.12 = (bf16[328,384]{1,0:T(8,128)(2,1)S(1)}, bf16[328,384]{1,0:T(8,128)(2,1)S(1)}, u32[]{:S(2)}, u32[]{:S(2)}) collective-permute-start(bf16[328,384]{1,0:T(8,128)(2,1)S(1)} %fusion.61), channel_id=1, source_target_pairs={{0,4},{4,0},{1,5},{5,1},{2,6},{6,2},{3,7},{7,3},{8,12},{12,8},{9,1... | collective-permute-start | bytes 755720 | tf_op jit(solution)/shard_map/ppermute | solution.py:109
  118.7 11.4 %collective-permute-start.13 = (bf16[656,384]{1,0:T(8,128)(2,1)}, bf16[656,384]{1,0:T(8,128)(2,1)S(1)}, u32[]{:S(2)}, u32[]{:S(2)}) collective-permute-start(bf16[656,384]{1,0:T(8,128)(2,1)} %get-tuple-element.57), channel_id=1, source_target_pairs={{0,2},{1,3},{2,0},{3,1},{4,6},{5,7},{6,4},{7,5},{8,10},{9,11},{10,... | collective-permute-start | bytes 1511432 | tf_op jit(solution)/shard_map/ppermute | solution.py:109
  121.6 21.6 %all-to-all-start.2 = ((bf16[4,96,1,4,2,128]{5,1,4,3,2,0:T(8,128)(2,1)}), bf16[4,96,1,4,2,128]{5,1,4,3,2,0:T(8,128)(2,1)S(1)}, u32[]{:S(2)}, u32[]{:S(2)}) async-start(bf16[4,96,1,4,2,128]{5,1,4,3,2,0:T(8,128)(2,1)} %copy.36), calls=%async_computation.2 | async-start | bytes 1572864 | tf_op jit(solution)/shard_map/all_to_all | solution.py:196
  130.6 12.7 %copy-start.7 = (f32[96]{0:T(128)S(1)}, f32[96]{0:T(128)}, u32[]{:S(2)}) copy-start(f32[96]{0:T(128)} %param.24) | copy-start | bytes 1156
  131.7 12.6 %collective-permute-start.14 = (bf16[1312,384]{1,0:T(8,128)(2,1)}, bf16[1312,384]{1,0:T(8,128)(2,1)S(1)}, u32[]{:S(2)}, u32[]{:S(2)}) collective-permute-start(bf16[1312,384]{1,0:T(8,128)(2,1)} %get-tuple-element.53), channel_id=1, source_target_pairs={{0,1},{1,0},{2,3},{3,2},{4,5},{5,4},{6,7},{7,6},{8,9},{9,8},{10,11... | collective-permute-start | bytes 3022856 | tf_op jit(solution)/shard_map/ppermute | solution.py:109
